TPU v7x, 256 devices: a whole 4x4x8 slice. The times are simulated.
256 devices in a mesh: gx: 8 (over z), gy: 4 (over y_lo, core), gz: 8 (over y_hi, x).
Axes of the slice: x: 4, y: 4 (y_hi: 2, y_lo: 2; y = y_hi * 2 + y_lo), z: 8, core: 2. Of those that a mesh axis runs over, the one named last changes fastest.
Arguments:
- state: bfloat16 [128, 64, 16, 8, 128], P('gx', 'gy', 'gz'), may hold values from -6 to 6
- cotangent: bfloat16 [128, 64, 16, 8, 128], P('gx', 'gy', 'gz'), may hold values from -6 to 6
- counts: int32 [8], P('gz'), may hold values from 1 to 2, 12 in all
- edge_weights: bfloat16 [2, 2, 128, 128], replicated, may hold values from -0.5 to 0.5
- node_in: bfloat16 [2, 256, 128], replicated, may hold values from -0.375 to 0.375
- node_out: bfloat16 [2, 128, 128], replicated, may hold values from -0.5 to 0.5
- biases: float32 [2, 2, 128], replicated, may hold values from -4 to 4
Outputs:
- state_grad: bfloat16 [128, 64, 16, 8, 128], P('gx', 'gy', 'gz')
- edge_grads: float32 [2, 2, 128, 128], replicated
- node_in_grad: float32 [2, 256, 128], replicated
- node_out_grad: float32 [2, 128, 128], replicated
- bias_grads: float32 [2, 2, 128], replicated
Inputs may be any that keep to these rules, and one draw needn't show every extreme that they name: The counts sum to 12; index k of gz holds the element layers that follow those of smaller indices.
All inputs are finite; a program needn't handle non-finite values. No bound on the sum of `counts` on one device may be relied on, other than what follows from the above.
Results may differ from a plain program's by a relative error of at most 0.012.
The roundings to bfloat16 on the way count: a program that leaves them out, or rounds other values in their place, can miss the bound.
Values sent between devices are 32-bit elements; how exact they have to be, the bound alone decides.
A program may use at most 128 MiB of HBM per device.

v0:
```python
import math
import jax
import jax.numpy as jnp
from jax import lax
from jax.sharding import PartitionSpec as P

edge_dims = (1, 3, 5)


def with_halo(cells, sides, width):
    for axis, dim in sides:
        count = lax.axis_size(axis)
        ends = count - 1
        head = lax.slice_in_dim(cells, 0, width, axis=dim)
        tail = lax.slice_in_dim(cells, cells.shape[dim] - width, cells.shape[dim], axis=dim)
        cells = jnp.concatenate(
            [
                lax.ppermute(tail, axis, [(i, (i + 1) % count) for i in range(ends)]),
                cells,
                lax.ppermute(head, axis, [((i + 1) % count, i) for i in range(ends)]),
            ],
            axis=dim,
        )
    return cells


def slice_along(array, start, stop, dim_no):
    return lax.slice_in_dim(array, start, stop, axis=dim_no)


def matmul_rows(left, weight):
    flattened = left.reshape(-1, left.shape[-1])
    product = jnp.dot(flattened, weight, preferred_element_type=jnp.float32)
    return product.reshape(left.shape[:-1] + (weight.shape[-1],))


def cross_rows(left, right):
    return lax.dot_general(
        left.reshape(-1, left.shape[-1]),
        right.reshape(-1, right.shape[-1]),
        (((0,), (0,)), ((), ())),
        preferred_element_type=jnp.float32,
    )


def spread_diff(values, dim_no):
    zero_row = jnp.zeros_like(slice_along(values, 0, 1, dim_no))
    return jnp.concatenate([zero_row, values], dim_no) - jnp.concatenate([values, zero_row], dim_no)


def silu_slope(values):
    sig_value = jax.nn.sigmoid(values)
    return sig_value * (1.0 + values * (1.0 - sig_value))


def edges_forward(features, weight_one, weight_two, bias_edge):
    widened = features.astype(jnp.float32)
    messages = jnp.zeros(features.shape, jnp.float32)
    stored = []
    for dim_no in edge_dims:
        length = features.shape[dim_no]
        differ = (
            slice_along(widened, 1, length, dim_no) - slice_along(widened, 0, length - 1, dim_no)
        ).astype(jnp.bfloat16)
        before = matmul_rows(differ, weight_one) + bias_edge
        active = jax.nn.silu(before).astype(jnp.bfloat16)
        messages = messages + spread_diff(matmul_rows(active, weight_two), dim_no)
        stored.append((differ, before, active))
    return (messages, stored)


def edges_backward(grad_msg, stored, weight_one, weight_two):
    feat_width = grad_msg.shape[-1]
    grad_feat = jnp.zeros(grad_msg.shape, jnp.float32)
    grad_one = jnp.zeros((feat_width, feat_width), jnp.float32)
    grad_two = jnp.zeros((feat_width, feat_width), jnp.float32)
    grad_bias = jnp.zeros((feat_width,), jnp.float32)
    for dim_no, entry in zip(edge_dims, stored):
        differ, before, active = entry
        length = grad_msg.shape[dim_no]
        grad_out = (
            slice_along(grad_msg, 1, length, dim_no) - slice_along(grad_msg, 0, length - 1, dim_no)
        ).astype(jnp.bfloat16)
        grad_two = grad_two + cross_rows(active, grad_out)
        grad_pre = (matmul_rows(grad_out, weight_two.T) * silu_slope(before)).astype(jnp.bfloat16)
        grad_one = grad_one + cross_rows(differ, grad_pre)
        grad_bias = grad_bias + jnp.sum(grad_pre.astype(jnp.float32).reshape(-1, feat_width), 0)
        grad_feat = grad_feat + spread_diff(matmul_rows(grad_pre, weight_one.T), dim_no)
    return (grad_feat, grad_one, grad_two, grad_bias)


def node_forward(features, summed, weight_in, weight_out, bias_node):
    joined = jnp.concatenate([features, summed.astype(jnp.bfloat16)], -1)
    before = matmul_rows(joined, weight_in) + bias_node
    active = jax.nn.silu(before).astype(jnp.bfloat16)
    result = (features.astype(jnp.float32) + matmul_rows(active, weight_out)).astype(jnp.bfloat16)
    return (result, (joined, before, active))


def node_backward(grad_next, stored, weight_in, weight_out):
    joined, before, active = stored
    feat_width = grad_next.shape[-1]
    grad_out_w = cross_rows(active, grad_next)
    grad_pre = (matmul_rows(grad_next, weight_out.T) * silu_slope(before)).astype(jnp.bfloat16)
    grad_in_w = cross_rows(joined, grad_pre)
    grad_bias = jnp.sum(grad_pre.astype(jnp.float32).reshape(-1, feat_width), 0)
    grad_joined = matmul_rows(grad_pre, weight_in.T)
    grad_feat = grad_next.astype(jnp.float32) + grad_joined[..., :feat_width]
    return (grad_feat, grad_joined[..., feat_width:], grad_in_w, grad_out_w, grad_bias)


def couple(array, elem_dim, node_dim):
    moved = jnp.moveaxis(array, (elem_dim, node_dim), (0, 1))
    front_face = moved[:, 0]
    back_face = moved[:, -1]
    zero_face = jnp.zeros_like(front_face[:1])
    new_front = front_face + jnp.concatenate([zero_face, back_face[:-1]], 0)
    new_back = back_face + jnp.concatenate([front_face[1:], zero_face], 0)
    joined = jnp.concatenate([new_front[:, None], moved[:, 1:-1], new_back[:, None]], 1)
    return jnp.moveaxis(joined, (0, 1), (elem_dim, node_dim))


def local_couple(values, dim_no, nodes_edge):
    full_shape = values.shape
    elems_here = full_shape[dim_no] // nodes_edge
    split_shape = full_shape[:dim_no] + (elems_here, nodes_edge) + full_shape[dim_no + 1 :]
    return couple(values.reshape(split_shape), dim_no, dim_no + 1).reshape(full_shape)


def fold_rim(extended, dim_no):
    inner_len = extended.shape[dim_no] - 2
    core_rows = slice_along(extended, 1, inner_len + 1, dim_no)
    front_row = slice_along(core_rows, 0, 1, dim_no) + slice_along(extended, 0, 1, dim_no)
    back_row = slice_along(core_rows, inner_len - 1, inner_len, dim_no) + slice_along(
        extended, inner_len + 1, inner_len + 2, dim_no
    )
    return jnp.concatenate(
        [front_row, slice_along(core_rows, 1, inner_len - 1, dim_no), back_row], dim_no
    )


def on_device(state, cotangent, counts, edge_weights, node_in, node_out, biases):
    nodes_edge = state.shape[3]
    span_x = state.shape[0]
    span_y = state.shape[1]
    elems_x = span_x // nodes_edge
    elems_y = span_y // nodes_edge
    slot_count = state.shape[2]
    grid_shape = state.shape[:4]
    filled = counts[0]
    slot_ids = jnp.arange(slot_count, dtype=jnp.int32)
    node_ids = jnp.arange(nodes_edge, dtype=jnp.int32)
    live_mask = (slot_ids < filled).astype(jnp.float32)[None, None, :, None, None]

    def edge_mult(position, axis_len, elems_here):
        place = jnp.arange(elems_here * nodes_edge, dtype=jnp.int32)
        node_here = place % nodes_edge
        elem_global = position * elems_here + place // nodes_edge
        front_pair = ((node_here == 0) & (elem_global > 0)).astype(jnp.float32)
        back_pair = (
            (node_here == nodes_edge - 1) & (elem_global < elems_here * axis_len - 1)
        ).astype(jnp.float32)
        return 1.0 + front_pair + back_pair

    mult_x = edge_mult(lax.axis_index("gx"), lax.axis_size("gx"), elems_x)
    mult_y = edge_mult(lax.axis_index("gy"), lax.axis_size("gy"), elems_y)
    index_z = lax.axis_index("gz")
    size_z = lax.axis_size("gz")
    lower_mult = ((slot_ids > 0) | (index_z > 0)).astype(jnp.float32)
    upper_mult = ((slot_ids < filled - 1) | (index_z < size_z - 1)).astype(jnp.float32)
    mult_z = (
        1.0
        + (node_ids == 0).astype(jnp.float32)[None, :] * lower_mult[:, None]
        + (node_ids == nodes_edge - 1).astype(jnp.float32)[None, :] * upper_mult[:, None]
    )
    copies = (
        mult_x[:, None, None, None, None]
        * mult_y[None, :, None, None, None]
        * mult_z[None, None, :, :, None]
    )

    def couple_all(values):
        inner = local_couple(local_couple(values, 0, nodes_edge), 1, nodes_edge)
        extended = with_halo(inner, (("gx", 0), ("gy", 1)), 1)
        coupled = fold_rim(fold_rim(extended, 0), 1)
        top_faces = coupled[:, :, :, -1]
        bottom_faces = coupled[:, :, :, 0]
        top_used = lax.dynamic_index_in_dim(top_faces, filled - 1, 2, keepdims=False)
        rim_pair = jnp.stack([bottom_faces[:, :, 0], top_used], 2)
        rim_ext = with_halo(rim_pair, (("gz", 2),), 1)
        from_below = rim_ext[:, :, 0]
        from_above = rim_ext[:, :, 3]
        below_add = jnp.concatenate([from_below[:, :, None], top_faces[:, :, :-1]], 2)
        last_slot = (slot_ids == filled - 1).astype(jnp.float32)[None, None, :, None]
        above_add = (
            jnp.concatenate([bottom_faces[:, :, 1:], jnp.zeros_like(bottom_faces[:, :, :1])], 2)
            + last_slot * from_above[:, :, None]
        )
        result = jnp.concatenate(
            [
                (bottom_faces + below_add)[:, :, :, None],
                coupled[:, :, :, 1:-1],
                (top_faces + above_add)[:, :, :, None],
            ],
            3,
        )
        return result * live_mask

    def to_cells(array):
        return array.reshape(
            (elems_x, nodes_edge, elems_y, nodes_edge, slot_count, nodes_edge, array.shape[-1])
        )

    def to_grid(array):
        return array.reshape(grid_shape + (array.shape[-1],))

    features = state
    grad_next = cotangent * live_mask.astype(jnp.bfloat16)
    saved = []
    for layer_no in range(2):
        messages, edge_store = edges_forward(
            to_cells(features),
            edge_weights[layer_no, 0],
            edge_weights[layer_no, 1],
            biases[layer_no, 0],
        )
        summed = couple_all(to_grid(messages) * live_mask) / copies
        result, node_store = node_forward(
            features, summed, node_in[layer_no], node_out[layer_no], biases[layer_no, 1]
        )
        saved.append((edge_store, node_store))
        features = result
    per_layer = [None, None]
    for layer_no in (1, 0):
        edge_store, node_store = saved[layer_no]
        grad_feat, grad_sum, grad_in_w, grad_out_w, grad_node_b = node_backward(
            grad_next, node_store, node_in[layer_no], node_out[layer_no]
        )
        grad_msg = couple_all(grad_sum / copies * live_mask)
        grad_edge, grad_one, grad_two, grad_edge_b = edges_backward(
            to_cells(grad_msg), edge_store, edge_weights[layer_no, 0], edge_weights[layer_no, 1]
        )
        grad_next = (grad_feat + to_grid(grad_edge)).astype(jnp.bfloat16)
        local_terms = (
            jnp.stack([grad_one, grad_two]),
            grad_in_w,
            grad_out_w,
            jnp.stack([grad_edge_b, grad_node_b]),
        )
        per_layer[layer_no] = local_terms
    stacked = tuple(
        (jnp.stack([per_layer[0][pos_no], per_layer[1][pos_no]]) for pos_no in range(4))
    )
    stacked = lax.psum(stacked, ("gx", "gy", "gz"))
    layers_all = 3 * slot_count * size_z // 4
    nodes_all = (
        nodes_edge**3 * elems_x * lax.axis_size("gx") * elems_y * lax.axis_size("gy") * layers_all
    )
    grad_scale = 1.0 / math.sqrt(nodes_all)
    state_grad = grad_next * live_mask.astype(jnp.bfloat16)
    return (
        state_grad,
        stacked[0] * grad_scale,
        stacked[1] * grad_scale,
        stacked[2] * grad_scale,
        stacked[3] * grad_scale,
    )


def solution(mesh):
    return jax.shard_map(
        on_device,
        mesh=mesh,
        in_specs=(
            P("gx", "gy", "gz", None, None),
            P("gx", "gy", "gz", None, None),
            P("gz"),
            P(),
            P(),
            P(),
            P(),
        ),
        out_specs=(P("gx", "gy", "gz", None, None), P(), P(), P(), P()),
        check_vma=False,
    )
```

profile of v0, /device:TPU:1, one launch (start us, length us, event | category | flops | bytes accessed | tf_op | source)
XLA Modules:
  0.0 601.1 jit_solution(5968325419626531154)
XLA Ops:
  12.3 1.9 multiply_convert_fusion.14
  15.5 1.8 multiply_convert_fusion.15
  18.3 1.7 fusion.24
  20.0 1.8 multiply_convert_fusion.13
  27.5 4.4 collective-permute-start
  33.2 2.4 copy_bitcast_fusion.7
  35.6 2.9 collective-permute-done.1
  38.5 1.8 pad_maximum_fusion.49
  40.3 4.7 collective-permute-start.2
  45.0 2.1 collective-permute-start.3
  47.4 4.4 collective-permute-done.3
  56.4 3.1 collective-permute-start.4
  63.2 4.5 collective-permute-done.5
  68.5 1.7 fusion.13
  70.3 2.1 multiply_convert_fusion.3
  74.4 1.8 multiply_convert_fusion.11
  77.7 1.7 fusion.23
  79.4 1.8 multiply_convert_fusion.10
  88.6 3.6 collective-permute-start.6
  94.8 5.2 collective-permute-done.7
  100.2 4.2 collective-permute-start.8
  104.4 1.9 collective-permute-start.9
  106.5 4.4 collective-permute-done.9
  112.7 3.6 collective-permute-start.10
  116.4 1.9 collective-permute-done.10
  121.6 3.5 collective-permute-done.11
  133.8 4.6 collective-permute-start.12
  140.9 4.1 collective-permute-done.13
  145.3 4.2 collective-permute-start.14
  149.5 1.9 collective-permute-start.15
  152.4 3.6 collective-permute-done.15
  157.7 5.7 collective-permute-start.16
  168.5 3.4 collective-permute-done.17
  192.4 3.6 collective-permute-start.18
  199.0 3.5 collective-permute-done.19
  202.7 4.2 collective-permute-start.20
  206.9 1.9 collective-permute-start.21
  209.5 3.8 collective-permute-done.21
  215.2 7.3 %collective-permute-start.22 = (f32[16,16,1,128]{3,1,0,2:T(8,128)S(1)}, f32[16,16,1,128]{3,1,0,2:T(8,128)S(1)}, u32[]{:S(2)}, u32[]{:S(2)}) collective-permute-start(f32[16,16,1,128]{3,1,0,2:T(8,128)S(1)} %dynamic-slice_bitcast_fusion), channel_id=1, source_target_pairs={{0,1},{1,2},{2,3},{3,4},{4,5},{5,6},{6,7},{8,9},{9,10},{10,11},{11... | collective-permute-start | bytes 393224 | tf_op jit(solution)/shard_map/ppermute | solution.py:18
  227.5 3.4 collective-permute-done.23
  237.5 1.7 fusion.129
  244.4 1.8 convert_reduce_fusion.7
  246.3 84.3 %psum.31 = f32[2,2,128]{2,1,0:T(2,128)S(1)} all-reduce(f32[2,2,128]{2,1,0:T(2,128)S(1)} %pad_maximum_fusion.51), channel_id=1, replica_groups=mesh['gx'=8,'gy'=4,'gz'=8] {'gx','gy','gz'}, use_global_device_ids=true, to_apply=%region_11.12 | all-reduce | flops 512 | bytes 4096 | tf_op jit(solution)/shard_map/psum | solution.py:254
  331.2 2.8 fusion.131
  336.7 4.3 subtract_add_fusion
  342.6 246.3 %all-reduce.47.cloned.1.call-done = (f32[2,2,128,128]{3,2,1,0:T(8,128)}, f32[2,256,128]{2,1,0:T(8,128)}, f32[2,128,128]{2,1,0:T(8,128)}) async-done(((f32[2,2,128,128]{3,2,1,0:T(8,128)}, f32[2,256,128]{2,1,0:T(8,128)}, f32[2,128,128]{2,1,0:T(8,128)}), (f32[2,2,128,128]{3,2,1,0:T(8,128)}, f32[2,256,128]{2,1,0:T(8,128)}, f32[2,128,128]{2,1,0:T(8,128)})) %all-reduce.47.cloned.1.call-update) | async-done | bytes 655376 | tf_op jit(solution)/shard_map/psum | solution.py:254
  588.9 1.7 broadcast_multiply_fusion.3
  592.1 1.7 broadcast_multiply_fusion.2
  (316 shorter events, 109.3 us)
Async XLA Ops:
  7.2 581.7 %all-reduce.47.cloned.1.call-start = ((), (), s32[]{:S(2)}) async-start(), calls=%async_computation | async-start | bytes 1310720 | tf_op jit(solution)/shard_map/psum | solution.py:254
  8.9 6.6 %copy-start.14 = (bf16[2,7,2,8,2,8,128]{6,5,4,3,2,1,0:T(8,128)(2,1)}, bf16[2,7,2,8,2,8,128]{6,5,4,3,2,1,0:T(8,128)(2,1)S(1)}, u32[]{:S(2)}) copy-start(bf16[2,7,2,8,2,8,128]{6,5,4,3,2,1,0:T(8,128)(2,1)S(1)} %fusion.22) | copy-start | bytes 2752516
  8.9 1.6 copy-start
  10.5 1.8 copy-start.18
  10.5 1.8 copy-start.9
  12.3 7.7 %copy-start.28 = (f32[128]{0:T(128)}, f32[128]{0:T(128)S(1)}, u32[]{:S(2)}) copy-start(f32[128]{0:T(128)S(1)} %get-tuple-element.80) | copy-start | bytes 1540
  20.0 1.8 copy-start.12
  25.7 7.5 %copy-start.4 = (f32[2,16,2,8,128]{4,0,3,2,1:T(2,128)}, f32[2,16,2,8,128]{4,0,3,2,1:T(2,128)S(1)}, u32[]{:S(2)}) copy-start(f32[2,16,2,8,128]{4,0,3,2,1:T(2,128)S(1)} %copy_add_fusion.4) | copy-start | bytes 786436
  27.5 8.1 %collective-permute-start = (f32[1,16,2,8,128]{4,1,0,3,2:T(8,128)}, f32[1,16,2,8,128]{4,1,0,3,2:T(8,128)S(1)}, u32[]{:S(2)}, u32[]{:S(2)}) collective-permute-start(f32[1,16,2,8,128]{4,1,0,3,2:T(8,128)} %get-tuple-element.56), channel_id=1, source_target_pairs={{0,32},{32,64},{64,96},{96,128},{128,160},{160,192},{192,224},{1,3... | collective-permute-start | bytes 393224 | tf_op jit(solution)/shard_map/ppermute | solution.py:18
  31.8 6.7 %collective-permute-start.1 = (f32[1,16,2,8,128]{4,1,0,3,2:T(8,128)}, f32[1,16,2,8,128]{4,1,0,3,2:T(8,128)}, u32[]{:S(2)}, u32[]{:S(2)}) collective-permute-start(f32[1,16,2,8,128]{4,1,0,3,2:T(8,128)} %get-tuple-element.57), channel_id=1, source_target_pairs={{32,0},{64,32},{96,64},{128,96},{160,128},{192,160},{224,192},{33,... | collective-permute-start | bytes 393224 | tf_op jit(solution)/shard_map/ppermute | solution.py:20
  40.3 7.1 %collective-permute-start.2 = (f32[18,1,2,8,128]{4,1,0,3,2:T(1,128)}, f32[18,1,2,8,128]{4,1,0,3,2:T(1,128)S(1)}, u32[]{:S(2)}, u32[]{:S(2)}) collective-permute-start(f32[18,1,2,8,128]{4,1,0,3,2:T(1,128)} %get-tuple-element.30), channel_id=1, source_target_pairs={{0,8},{8,16},{16,24},{1,9},{9,17},{17,25},{2,10},{10,18},{18,26},{... | collective-permute-start | bytes 442376 | tf_op jit(solution)/shard_map/ppermute | solution.py:18
  45.0 6.8 %collective-permute-start.3 = (f32[18,1,2,8,128]{4,1,0,3,2:T(1,128)}, f32[18,1,2,8,128]{4,1,0,3,2:T(1,128)}, u32[]{:S(2)}, u32[]{:S(2)}) collective-permute-start(f32[18,1,2,8,128]{4,1,0,3,2:T(1,128)} %get-tuple-element.31), channel_id=1, source_target_pairs={{8,0},{16,8},{24,16},{9,1},{17,9},{25,17},{10,2},{18,10},{26,18},{... | collective-permute-start | bytes 442376 | tf_op jit(solution)/shard_map/ppermute | solution.py:20
  47.4 5.9 copy-start.5
  56.4 5.1 collective-permute-start.4
  61.6 6.1 %collective-permute-start.5 = (f32[16,16,1,128]{3,1,0,2:T(8,128)S(1)}, f32[16,16,1,128]{3,1,0,2:T(8,128)S(1)}, u32[]{:S(2)}, u32[]{:S(2)}) collective-permute-start(f32[16,16,1,128]{3,1,0,2:T(8,128)S(1)} %get-tuple-element.76), channel_id=1, source_target_pairs={{1,0},{2,1},{3,2},{4,3},{5,4},{6,5},{7,6},{9,8},{10,9},{11,10},{12... | collective-permute-start | bytes 393224 | tf_op jit(solution)/shard_map/ppermute | solution.py:20
  68.5 1.8 copy-start.25
  68.5 1.8 copy-start.30
  70.3 2.1 copy-start.26
  88.6 6.2 %collective-permute-start.6 = (f32[1,16,2,8,128]{4,1,0,2,3:T(8,128)S(1)}, f32[1,16,2,8,128]{4,1,0,2,3:T(8,128)S(1)}, u32[]{:S(2)}, u32[]{:S(2)}) collective-permute-start(f32[1,16,2,8,128]{4,1,0,2,3:T(8,128)S(1)} %get-tuple-element.48), channel_id=1, source_target_pairs={{0,32},{32,64},{64,96},{96,128},{128,160},{160,192},{192,224},{1,3... | collective-permute-start | bytes 393224 | tf_op jit(solution)/shard_map/ppermute | solution.py:18
  92.2 7.8 %collective-permute-start.7 = (f32[1,16,2,8,128]{4,1,0,2,3:T(8,128)S(1)}, f32[1,16,2,8,128]{4,1,0,2,3:T(8,128)S(1)}, u32[]{:S(2)}, u32[]{:S(2)}) collective-permute-start(f32[1,16,2,8,128]{4,1,0,2,3:T(8,128)S(1)} %get-tuple-element.49), channel_id=1, source_target_pairs={{32,0},{64,32},{96,64},{128,96},{160,128},{192,160},{224,192},{33,... | collective-permute-start | bytes 393224 | tf_op jit(solution)/shard_map/ppermute | solution.py:20
  100.2 6.3 %collective-permute-start.8 = (f32[18,1,2,8,128]{4,1,0,2,3:T(1,128)S(1)}, f32[18,1,2,8,128]{4,1,0,2,3:T(1,128)S(1)}, u32[]{:S(2)}, u32[]{:S(2)}) collective-permute-start(f32[18,1,2,8,128]{4,1,0,2,3:T(1,128)S(1)} %get-tuple-element.28), channel_id=1, source_target_pairs={{0,8},{8,16},{16,24},{1,9},{9,17},{17,25},{2,10},{10,18},{18,26},{... | collective-permute-start | bytes 442376 | tf_op jit(solution)/shard_map/ppermute | solution.py:18
  104.4 6.5 %collective-permute-start.9 = (f32[18,1,2,8,128]{4,1,0,2,3:T(1,128)S(1)}, f32[18,1,2,8,128]{4,1,0,2,3:T(1,128)S(1)}, u32[]{:S(2)}, u32[]{:S(2)}) collective-permute-start(f32[18,1,2,8,128]{4,1,0,2,3:T(1,128)S(1)} %get-tuple-element.29), channel_id=1, source_target_pairs={{8,0},{16,8},{24,16},{9,1},{17,9},{25,17},{10,2},{18,10},{26,18},{... | collective-permute-start | bytes 442376 | tf_op jit(solution)/shard_map/ppermute | solution.py:20
  112.7 5.6 collective-permute-start.10
  119.0 6.1 %collective-permute-start.11 = (f32[16,16,1,128]{3,2,1,0:T(1,128)S(1)}, f32[16,16,1,128]{3,2,1,0:T(1,128)S(1)}, u32[]{:S(2)}, u32[]{:S(2)}) collective-permute-start(f32[16,16,1,128]{3,2,1,0:T(1,128)S(1)} %get-tuple-element.74), channel_id=1, source_target_pairs={{1,0},{2,1},{3,2},{4,3},{5,4},{6,5},{7,6},{9,8},{10,9},{11,10},{12... | collective-permute-start | bytes 393224 | tf_op jit(solution)/shard_map/ppermute | solution.py:20
  133.8 7.2 %collective-permute-start.12 = (f32[1,16,2,8,128]{4,1,0,3,2:T(8,128)S(1)}, f32[1,16,2,8,128]{4,1,0,3,2:T(8,128)S(1)}, u32[]{:S(2)}, u32[]{:S(2)}) collective-permute-start(f32[1,16,2,8,128]{4,1,0,3,2:T(8,128)S(1)} %get-tuple-element.40), channel_id=1, source_target_pairs={{0,32},{32,64},{64,96},{96,128},{128,160},{160,192},{192,224},{1,3... | collective-permute-start | bytes 393224 | tf_op jit(solution)/shard_map/ppermute | solution.py:18
  138.4 6.7 %collective-permute-start.13 = (f32[1,16,2,8,128]{4,1,0,3,2:T(8,128)S(1)}, f32[1,16,2,8,128]{4,1,0,3,2:T(8,128)S(1)}, u32[]{:S(2)}, u32[]{:S(2)}) collective-permute-start(f32[1,16,2,8,128]{4,1,0,3,2:T(8,128)S(1)} %get-tuple-element.41), channel_id=1, source_target_pairs={{32,0},{64,32},{96,64},{128,96},{160,128},{192,160},{224,192},{33,... | collective-permute-start | bytes 393224 | tf_op jit(solution)/shard_map/ppermute | solution.py:20
  145.3 7.1 %collective-permute-start.14 = (f32[18,1,2,8,128]{4,1,0,3,2:T(1,128)S(1)}, f32[18,1,2,8,128]{4,1,0,3,2:T(1,128)S(1)}, u32[]{:S(2)}, u32[]{:S(2)}) collective-permute-start(f32[18,1,2,8,128]{4,1,0,3,2:T(1,128)S(1)} %get-tuple-element.24), channel_id=1, source_target_pairs={{0,8},{8,16},{16,24},{1,9},{9,17},{17,25},{2,10},{10,18},{18,26},{... | collective-permute-start | bytes 442376 | tf_op jit(solution)/shard_map/ppermute | solution.py:18
  149.5 6.5 %collective-permute-start.15 = (f32[18,1,2,8,128]{4,1,0,3,2:T(1,128)S(1)}, f32[18,1,2,8,128]{4,1,0,3,2:T(1,128)S(1)}, u32[]{:S(2)}, u32[]{:S(2)}) collective-permute-start(f32[18,1,2,8,128]{4,1,0,3,2:T(1,128)S(1)} %get-tuple-element.25), channel_id=1, source_target_pairs={{8,0},{16,8},{24,16},{9,1},{17,9},{25,17},{10,2},{18,10},{26,18},{... | collective-permute-start | bytes 442376 | tf_op jit(solution)/shard_map/ppermute | solution.py:20
  157.7 7.6 %collective-permute-start.16 = (f32[16,16,1,128]{3,1,0,2:T(8,128)S(1)}, f32[16,16,1,128]{3,1,0,2:T(8,128)S(1)}, u32[]{:S(2)}, u32[]{:S(2)}) collective-permute-start(f32[16,16,1,128]{3,1,0,2:T(8,128)S(1)} %dynamic-slice_bitcast_fusion.1), channel_id=1, source_target_pairs={{0,1},{1,2},{2,3},{3,4},{4,5},{5,6},{6,7},{8,9},{9,10},{10,11},{11... | collective-permute-start | bytes 393224 | tf_op jit(solution)/shard_map/ppermute | solution.py:18
  165.5 6.4 %collective-permute-start.17 = (f32[16,16,1,128]{3,1,0,2:T(8,128)S(1)}, f32[16,16,1,128]{3,1,0,2:T(8,128)S(1)}, u32[]{:S(2)}, u32[]{:S(2)}) collective-permute-start(f32[16,16,1,128]{3,1,0,2:T(8,128)S(1)} %get-tuple-element.70), channel_id=1, source_target_pairs={{1,0},{2,1},{3,2},{4,3},{5,4},{6,5},{7,6},{9,8},{10,9},{11,10},{12... | collective-permute-start | bytes 393224 | tf_op jit(solution)/shard_map/ppermute | solution.py:20
  173.7 1.5 copy-start.36
  177.0 1.5 copy-start.37
  182.8 1.6 copy-start.38
  187.3 2.0 copy-start.2
  192.4 6.6 %collective-permute-start.18 = (f32[1,16,2,8,128]{4,1,0,3,2:T(8,128)S(1)}, f32[1,16,2,8,128]{4,1,0,3,2:T(8,128)S(1)}, u32[]{:S(2)}, u32[]{:S(2)}) collective-permute-start(f32[1,16,2,8,128]{4,1,0,3,2:T(8,128)S(1)} %get-tuple-element.32), channel_id=1, source_target_pairs={{0,32},{32,64},{64,96},{96,128},{128,160},{160,192},{192,224},{1,3... | collective-permute-start | bytes 393224 | tf_op jit(solution)/shard_map/ppermute | solution.py:18
  196.1 6.4 %collective-permute-start.19 = (f32[1,16,2,8,128]{4,1,0,3,2:T(8,128)S(1)}, f32[1,16,2,8,128]{4,1,0,3,2:T(8,128)S(1)}, u32[]{:S(2)}, u32[]{:S(2)}) collective-permute-start(f32[1,16,2,8,128]{4,1,0,3,2:T(8,128)S(1)} %get-tuple-element.33), channel_id=1, source_target_pairs={{32,0},{64,32},{96,64},{128,96},{160,128},{192,160},{224,192},{33,... | collective-permute-start | bytes 393224 | tf_op jit(solution)/shard_map/ppermute | solution.py:20
  202.7 6.9 %collective-permute-start.20 = (f32[18,1,2,8,128]{4,1,0,3,2:T(1,128)S(1)}, f32[18,1,2,8,128]{4,1,0,3,2:T(1,128)S(1)}, u32[]{:S(2)}, u32[]{:S(2)}) collective-permute-start(f32[18,1,2,8,128]{4,1,0,3,2:T(1,128)S(1)} %get-tuple-element.22), channel_id=1, source_target_pairs={{0,8},{8,16},{16,24},{1,9},{9,17},{17,25},{2,10},{10,18},{18,26},{... | collective-permute-start | bytes 442376 | tf_op jit(solution)/shard_map/ppermute | solution.py:18
  206.9 6.5 %collective-permute-start.21 = (f32[18,1,2,8,128]{4,1,0,3,2:T(1,128)S(1)}, f32[18,1,2,8,128]{4,1,0,3,2:T(1,128)S(1)}, u32[]{:S(2)}, u32[]{:S(2)}) collective-permute-start(f32[18,1,2,8,128]{4,1,0,3,2:T(1,128)S(1)} %get-tuple-element.23), channel_id=1, source_target_pairs={{8,0},{16,8},{24,16},{9,1},{17,9},{25,17},{10,2},{18,10},{26,18},{... | collective-permute-start | bytes 442376 | tf_op jit(solution)/shard_map/ppermute | solution.py:20
  215.2 9.2 %collective-permute-start.22 = (f32[16,16,1,128]{3,1,0,2:T(8,128)S(1)}, f32[16,16,1,128]{3,1,0,2:T(8,128)S(1)}, u32[]{:S(2)}, u32[]{:S(2)}) collective-permute-start(f32[16,16,1,128]{3,1,0,2:T(8,128)S(1)} %dynamic-slice_bitcast_fusion), channel_id=1, source_target_pairs={{0,1},{1,2},{2,3},{3,4},{4,5},{5,6},{6,7},{8,9},{9,10},{10,11},{11... | collective-permute-start | bytes 393224 | tf_op jit(solution)/shard_map/ppermute | solution.py:18
  224.5 6.4 %collective-permute-start.23 = (f32[16,16,1,128]{3,1,0,2:T(8,128)S(1)}, f32[16,16,1,128]{3,1,0,2:T(8,128)S(1)}, u32[]{:S(2)}, u32[]{:S(2)}) collective-permute-start(f32[16,16,1,128]{3,1,0,2:T(8,128)S(1)} %get-tuple-element.68), channel_id=1, source_target_pairs={{1,0},{2,1},{3,2},{4,3},{5,4},{6,5},{7,6},{9,8},{10,9},{11,10},{12... | collective-permute-start | bytes 393224 | tf_op jit(solution)/shard_map/ppermute | solution.py:20
  232.2 11.2 %copy-start.22 = (bf16[2,7,2,8,2,8,128]{6,5,4,3,2,1,0:T(8,128)(2,1)}, bf16[2,7,2,8,2,8,128]{6,5,4,3,2,1,0:T(8,128)(2,1)S(1)}, u32[]{:S(2)}) copy-start(bf16[2,7,2,8,2,8,128]{6,5,4,3,2,1,0:T(8,128)(2,1)S(1)} %fusion.16) | copy-start | bytes 2752516
  233.7 1.5 copy-start.34
  237.5 1.7 copy-start.8
  239.2 1.5 copy-start.35
  242.9 1.5 copy-start.33
  330.6 3.4 copy-start.17
  330.6 3.4 copy-start.23
  336.7 4.4 copy-start.3
  (18 other events, 21.0 us)
Sparse Core Ops, SparseCore 0:
  336.8 251.9 all-reduce.46
where the time goes:
time: 610 us; the launch traced here: 601 us
  waiting for transfers between devices  300 us (49%)
  blocking collectives  84.3 us (14%)
  starting transfers between devices  71.9 us (12%)
  other arithmetic  53.6 us (9%)
  matrix products  43.4 us (7%)
  local copies, waits for them, and re-layouts  31.1 us (5%)
  between operations  17 us (3%)
    psum x1, waiting for transfers between devices, on_device(): stacked = lax.psum(stacked, ('gx', 'gy', 'gz'))  246 us
    psum x1, blocking collectives, on_device(): stacked = lax.psum(stacked, ('gx', 'gy', 'gz'))  84.3 us
    ppermute x12, starting transfers between devices, with_halo(): lax.ppermute(tail, axis, [(i, (i + 1) % count) for i in range(ends)])  53.2 us
    ppermute x12, waiting for transfers between devices, with_halo(): lax.ppermute(head, axis, [((i + 1) % count, i) for i in range(ends)])  46.7 us
    dot_general x31, matrix products, matmul_rows(): product = jnp.dot(flattened, weight, preferred_element_type=jnp.float32)  31.6 us
    ppermute x12, starting transfers between devices, with_halo(): lax.ppermute(head, axis, [((i + 1) % count, i) for i in range(ends)])  18.6 us
    unnamed x82, local copies, waits for them, and re-layouts  12.7 us
  transfers between devices with their start and end apart: 25, of which 21 were waited for; matrix products, arithmetic and copies ran while one was open for 3% of the time, Pallas kernels for 0%

commit v1 on v0

--- a/solution.py
+++ b/solution.py
@@ -251,7 +251,8 @@
     stacked = tuple(
         (jnp.stack([per_layer[0][pos_no], per_layer[1][pos_no]]) for pos_no in range(4))
     )
-    stacked = lax.psum(stacked, ("gx", "gy", "gz"))
+    partial = lax.psum(stacked, ("gy", "gz"))
+    stacked = lax.psum(partial, "gx")
     layers_all = 3 * slot_count * size_z // 4
     nodes_all = (
         nodes_edge**3 * elems_x * lax.axis_size("gx") * elems_y * lax.axis_size("gy") * layers_all

time: 610 us -> 480 us (0.79)
  the two profiles are of different devices: /device:TPU:1 before, /device:TPU:16 now
where the time goes in v1:
time: 480 us; the launch traced here: 471 us
  waiting for transfers between devices  185 us (39%)
  blocking collectives  93.8 us (20%)
  other arithmetic  56.9 us (12%)
  starting transfers between devices  51.9 us (11%)
  matrix products  36.2 us (8%)
  local copies, waits for them, and re-layouts  29.5 us (6%)
  between operations  17 us (4%)
    psum x1, waiting for transfers between devices, on_device(): partial = lax.psum(stacked, ('gy', 'gz'))  106 us
    psum x1, blocking collectives, on_device(): partial = lax.psum(stacked, ('gy', 'gz'))  76.3 us
    ppermute x12, waiting for transfers between devices, with_halo(): lax.ppermute(head, axis, [((i + 1) % count, i) for i in range(ends)])  45.9 us
    ppermute x12, waiting for transfers between devices, with_halo(): lax.ppermute(tail, axis, [(i, (i + 1) % count) for i in range(ends)])  33.6 us
    ppermute x12, starting transfers between devices, with_halo(): lax.ppermute(tail, axis, [(i, (i + 1) % count) for i in range(ends)])  33.2 us
    dot_general x31, matrix products, matmul_rows(): product = jnp.dot(flattened, weight, preferred_element_type=jnp.float32)  27.2 us
    ppermute x12, starting transfers between devices, with_halo(): lax.ppermute(head, axis, [((i + 1) % count, i) for i in range(ends)])  18.6 us
    psum x1, blocking collectives, on_device(): stacked = lax.psum(partial, 'gx')  17.4 us
  transfers between devices with their start and end apart: 26, of which 20 were waited for; matrix products, arithmetic and copies ran while one was open for 5% of the time, Pallas kernels for 0%

profile of v1, /device:TPU:16, one launch (start us, length us, event | category | flops | bytes accessed | tf_op | source)
XLA Modules:
  0.0 470.7 jit_solution(7676525129523347078)
XLA Ops:
  12.2 1.8 multiply_convert_fusion.14
  15.4 1.9 multiply_convert_fusion.15
  18.2 1.7 fusion.24
  20.0 1.8 multiply_convert_fusion.13
  28.5 3.8 collective-permute-start
  33.7 2.4 copy_bitcast_fusion.7
  36.0 3.6 collective-permute-done.1
  39.6 1.8 pad_maximum_fusion.49
  44.2 3.6 collective-permute-done.3
  52.5 3.4 collective-permute-start.4
  56.2 6.7 %collective-permute-done.4 = f32[16,16,1,128]{3,1,0,2:T(8,128)S(1)} collective-permute-done((f32[16,16,1,128]{3,1,0,2:T(8,128)S(1)}, f32[16,16,1,128]{3,1,0,2:T(8,128)S(1)}, u32[]{:S(2)}, u32[]{:S(2)}) %collective-permute-start.4) | collective-permute-done | bytes 131104 | tf_op jit(solution)/shard_map/ppermute | solution.py:18
  63.0 1.9 collective-permute-start.5
  65.3 4.6 collective-permute-done.5
  70.8 1.7 fusion.13
  77.5 1.7 fusion.23
  87.3 3.8 collective-permute-start.6
  94.6 5.5 %collective-permute-done.7 = f32[1,16,2,8,128]{4,1,0,2,3:T(8,128)S(1)} collective-permute-done((f32[1,16,2,8,128]{4,1,0,2,3:T(8,128)S(1)}, f32[1,16,2,8,128]{4,1,0,2,3:T(8,128)S(1)}, u32[]{:S(2)}, u32[]{:S(2)}) %collective-permute-start.7) | collective-permute-done | bytes 131104 | tf_op jit(solution)/shard_map/ppermute | solution.py:20
  100.3 2.1 collective-permute-start.8
  103.7 3.7 collective-permute-done.9
  109.4 1.9 collective-permute-start.10
  111.3 8.5 %collective-permute-done.10 = f32[16,16,1,128]{3,1,0,2:T(8,128)S(1)} collective-permute-done((f32[16,16,1,128]{3,1,0,2:T(8,128)S(1)}, f32[16,16,1,128]{3,1,0,2:T(8,128)S(1)}, u32[]{:S(2)}, u32[]{:S(2)}) %collective-permute-start.10) | collective-permute-done | bytes 131104 | tf_op jit(solution)/shard_map/ppermute | solution.py:18
  120.5 1.9 collective-permute-start.11
  123.8 3.6 collective-permute-done.11
  136.0 4.9 %collective-permute-start.12 = (f32[1,16,2,8,128]{4,1,0,3,2:T(8,128)S(1)}, f32[1,16,2,8,128]{4,1,0,3,2:T(8,128)S(1)}, u32[]{:S(2)}, u32[]{:S(2)}) collective-permute-start(f32[1,16,2,8,128]{4,1,0,3,2:T(8,128)S(1)} %get-tuple-element.43), channel_id=1, source_target_pairs={{0,32},{32,64},{64,96},{96,128},{128,160},{160,192},{192,224},{1,3... | collective-permute-start | bytes 393224 | tf_op jit(solution)/shard_map/ppermute | solution.py:18
  144.3 4.4 collective-permute-done.13
  148.9 2.2 collective-permute-start.14
  153.4 2.8 collective-permute-done.15
  158.0 1.9 collective-permute-start.16
  161.1 7.4 %collective-permute-done.16 = f32[16,16,1,128]{3,1,0,2:T(8,128)S(1)} collective-permute-done((f32[16,16,1,128]{3,1,0,2:T(8,128)S(1)}, f32[16,16,1,128]{3,1,0,2:T(8,128)S(1)}, u32[]{:S(2)}, u32[]{:S(2)}) %collective-permute-start.16) | collective-permute-done | bytes 131104 | tf_op jit(solution)/shard_map/ppermute | solution.py:18
  168.6 2.1 collective-permute-start.17
  172.2 3.2 collective-permute-done.17
  193.2 3.9 collective-permute-start.18
  200.6 4.7 collective-permute-done.19
  205.5 2.0 collective-permute-start.20
  209.5 2.9 collective-permute-done.21
  214.3 1.9 collective-permute-start.22
  217.3 7.5 %collective-permute-done.22 = f32[16,16,1,128]{3,1,0,2:T(8,128)S(1)} collective-permute-done((f32[16,16,1,128]{3,1,0,2:T(8,128)S(1)}, f32[16,16,1,128]{3,1,0,2:T(8,128)S(1)}, u32[]{:S(2)}, u32[]{:S(2)}) %collective-permute-start.22) | collective-permute-done | bytes 131104 | tf_op jit(solution)/shard_map/ppermute | solution.py:18
  224.9 2.2 collective-permute-start.23
  228.6 3.2 collective-permute-done.23
  242.4 1.8 fusion.44
  245.1 1.7 fusion.131
  249.3 5.8 %subtract_add_fusion = f32[2,8,2,8,2,8,128]{6,5,4,3,2,1,0:T(8,128)S(1)} fusion(f32[2,8,2,8,2,7,128]{6,5,4,3,2,1,0:T(8,128)} %fusion.44, f32[2,8,2,7,2,8,128]{6,5,4,3,2,1,0:T(8,128)} %fusion.129, f32[2,7,2,8,2,8,128]{6,5,4,3,2,1,0:T(8,128)} %fusion.131), kind=kLoop, calls=%fused_computation.58 | loop fusion | flops 2621440 | bytes 7602176 | tf_op jit(solution)/shard_map/add | solution.py:88
  255.1 105.9 %all-reduce.49.cloned.1.call-done = (f32[2,2,128,128]{3,2,1,0:T(8,128)}, f32[2,256,128]{2,1,0:T(8,128)}, f32[2,128,128]{2,1,0:T(8,128)}) async-done(((f32[2,2,128,128]{3,2,1,0:T(8,128)}, f32[2,256,128]{2,1,0:T(8,128)}, f32[2,128,128]{2,1,0:T(8,128)}), (f32[2,2,128,128]{3,2,1,0:T(8,128)}, f32[2,256,128]{2,1,0:T(8,128)}, f32[2,128,128]{2,1,0:T(8,128)})) %all-reduce.49.cloned.1.call-update) | async-done | bytes 655376 | tf_op jit(solution)/shard_map/psum | solution.py:254
  361.1 76.3 %psum.62 = f32[2,2,128]{2,1,0:T(2,128)S(1)} all-reduce(f32[2,2,128]{2,1,0:T(2,128)S(1)} %pad_maximum_fusion.51), channel_id=1, replica_groups=mesh['gx'=8,'gy'=4,'gz'=8] {'gy','gz'}, use_global_device_ids=true, to_apply=%region_14.15 | all-reduce | flops 512 | bytes 4096 | tf_op jit(solution)/shard_map/psum | solution.py:254
  437.4 17.4 %psum.63 = f32[2,2,128]{2,1,0:T(2,128)S(1)} all-reduce(f32[2,2,128]{2,1,0:T(2,128)S(1)} %psum.62), channel_id=1, replica_groups=mesh['gx'=8,'gy'=4,'gz'=8] {'gx'}, use_global_device_ids=true, to_apply=%region_15.16 | all-reduce | flops 512 | bytes 4096 | tf_op jit(solution)/shard_map/psum | solution.py:255
  455.4 3.0 fusion.43
  458.5 1.7 broadcast_multiply_fusion.3
  461.7 1.7 broadcast_multiply_fusion.2
  (306 shorter events, 107.5 us)
Async XLA Ops:
  7.2 353.9 %all-reduce.49.cloned.1.call-start = ((), (), s32[]{:S(2)}) async-start(), calls=%async_computation | async-start | bytes 1310720 | tf_op jit(solution)/shard_map/psum | solution.py:254
  8.9 6.5 %copy-start.15 = (bf16[2,7,2,8,2,8,128]{6,5,4,3,2,1,0:T(8,128)(2,1)}, bf16[2,7,2,8,2,8,128]{6,5,4,3,2,1,0:T(8,128)(2,1)S(1)}, u32[]{:S(2)}) copy-start(bf16[2,7,2,8,2,8,128]{6,5,4,3,2,1,0:T(8,128)(2,1)S(1)} %fusion.22) | copy-start | bytes 2752516
  8.9 1.6 copy-start
  10.5 1.7 copy-start.19
  10.5 1.2 copy-start.25
  10.5 1.7 copy-start.10
  12.2 7.7 %copy-start.26 = (f32[128]{0:T(128)}, f32[128]{0:T(128)S(1)}, u32[]{:S(2)}) copy-start(f32[128]{0:T(128)S(1)} %get-tuple-element.83) | copy-start | bytes 1540
  19.9 1.8 copy-start.13
  26.3 1.4 copy-start.1
  28.5 7.6 %collective-permute-start = (f32[1,16,2,8,128]{4,1,0,3,2:T(8,128)}, f32[1,16,2,8,128]{4,1,0,3,2:T(8,128)S(1)}, u32[]{:S(2)}, u32[]{:S(2)}) collective-permute-start(f32[1,16,2,8,128]{4,1,0,3,2:T(8,128)} %get-tuple-element.59), channel_id=1, source_target_pairs={{0,32},{32,64},{64,96},{96,128},{128,160},{160,192},{192,224},{1,3... | collective-permute-start | bytes 393224 | tf_op jit(solution)/shard_map/ppermute | solution.py:18
  32.3 7.3 %collective-permute-start.1 = (f32[1,16,2,8,128]{4,1,0,3,2:T(8,128)}, f32[1,16,2,8,128]{4,1,0,3,2:T(8,128)}, u32[]{:S(2)}, u32[]{:S(2)}) collective-permute-start(f32[1,16,2,8,128]{4,1,0,3,2:T(8,128)} %get-tuple-element.60), channel_id=1, source_target_pairs={{32,0},{64,32},{96,64},{128,96},{160,128},{192,160},{224,192},{33,... | collective-permute-start | bytes 393224 | tf_op jit(solution)/shard_map/ppermute | solution.py:20
  41.4 2.8 collective-permute-start.2
  42.7 5.1 %collective-permute-start.3 = (f32[18,1,2,8,128]{4,1,0,3,2:T(1,128)}, f32[18,1,2,8,128]{4,1,0,3,2:T(1,128)}, u32[]{:S(2)}, u32[]{:S(2)}) collective-permute-start(f32[18,1,2,8,128]{4,1,0,3,2:T(1,128)} %get-tuple-element.34), channel_id=1, source_target_pairs={{8,0},{16,8},{24,16},{9,1},{17,9},{25,17},{10,2},{18,10},{26,18},{... | collective-permute-start | bytes 442376 | tf_op jit(solution)/shard_map/ppermute | solution.py:20
  44.2 5.1 %copy-start.6 = (f32[18,1,2,8,128]{4,1,0,3,2:T(1,128)}, f32[18,1,2,8,128]{4,1,0,3,2:T(1,128)S(1)}, u32[]{:S(2)}) copy-start(f32[18,1,2,8,128]{4,1,0,3,2:T(1,128)S(1)} %collective-permute-done.2) | copy-start | bytes 442372
  52.5 10.5 %collective-permute-start.4 = (f32[16,16,1,128]{3,1,0,2:T(8,128)S(1)}, f32[16,16,1,128]{3,1,0,2:T(8,128)S(1)}, u32[]{:S(2)}, u32[]{:S(2)}) collective-permute-start(f32[16,16,1,128]{3,1,0,2:T(8,128)S(1)} %dynamic-slice_bitcast_fusion.3), channel_id=1, source_target_pairs={{0,1},{1,2},{2,3},{3,4},{4,5},{5,6},{6,7},{8,9},{9,10},{10,11},{11... | collective-permute-start | bytes 393224 | tf_op jit(solution)/shard_map/ppermute | solution.py:18
  63.0 6.9 %collective-permute-start.5 = (f32[16,16,1,128]{3,1,0,2:T(8,128)S(1)}, f32[16,16,1,128]{3,1,0,2:T(8,128)S(1)}, u32[]{:S(2)}, u32[]{:S(2)}) collective-permute-start(f32[16,16,1,128]{3,1,0,2:T(8,128)S(1)} %get-tuple-element.79), channel_id=1, source_target_pairs={{1,0},{2,1},{3,2},{4,3},{5,4},{6,5},{7,6},{9,8},{10,9},{11,10},{12... | collective-permute-start | bytes 393224 | tf_op jit(solution)/shard_map/ppermute | solution.py:20
  70.8 1.8 copy-start.23
  70.8 1.8 copy-start.28
  87.3 7.3 %collective-permute-start.6 = (f32[1,16,2,8,128]{4,1,0,2,3:T(8,128)S(1)}, f32[1,16,2,8,128]{4,1,0,2,3:T(8,128)S(1)}, u32[]{:S(2)}, u32[]{:S(2)}) collective-permute-start(f32[1,16,2,8,128]{4,1,0,2,3:T(8,128)S(1)} %get-tuple-element.51), channel_id=1, source_target_pairs={{0,32},{32,64},{64,96},{96,128},{128,160},{160,192},{192,224},{1,3... | collective-permute-start | bytes 393224 | tf_op jit(solution)/shard_map/ppermute | solution.py:18
  91.1 9.0 %collective-permute-start.7 = (f32[1,16,2,8,128]{4,1,0,2,3:T(8,128)S(1)}, f32[1,16,2,8,128]{4,1,0,2,3:T(8,128)S(1)}, u32[]{:S(2)}, u32[]{:S(2)}) collective-permute-start(f32[1,16,2,8,128]{4,1,0,2,3:T(8,128)S(1)} %get-tuple-element.52), channel_id=1, source_target_pairs={{32,0},{64,32},{96,64},{128,96},{160,128},{192,160},{224,192},{33,... | collective-permute-start | bytes 393224 | tf_op jit(solution)/shard_map/ppermute | solution.py:20
  100.3 3.4 collective-permute-start.8
  102.4 5.1 %collective-permute-start.9 = (f32[18,1,2,8,128]{4,1,0,2,3:T(1,128)S(1)}, f32[18,1,2,8,128]{4,1,0,2,3:T(1,128)S(1)}, u32[]{:S(2)}, u32[]{:S(2)}) collective-permute-start(f32[18,1,2,8,128]{4,1,0,2,3:T(1,128)S(1)} %get-tuple-element.32), channel_id=1, source_target_pairs={{8,0},{16,8},{24,16},{9,1},{17,9},{25,17},{10,2},{18,10},{26,18},{... | collective-permute-start | bytes 442376 | tf_op jit(solution)/shard_map/ppermute | solution.py:20
  109.4 10.5 %collective-permute-start.10 = (f32[16,16,1,128]{3,1,0,2:T(8,128)S(1)}, f32[16,16,1,128]{3,1,0,2:T(8,128)S(1)}, u32[]{:S(2)}, u32[]{:S(2)}) collective-permute-start(f32[16,16,1,128]{3,1,0,2:T(8,128)S(1)} %dynamic-slice_bitcast_fusion.2), channel_id=1, source_target_pairs={{0,1},{1,2},{2,3},{3,4},{4,5},{5,6},{6,7},{8,9},{9,10},{10,11},{11... | collective-permute-start | bytes 393224 | tf_op jit(solution)/shard_map/ppermute | solution.py:18
  120.5 6.9 %collective-permute-start.11 = (f32[16,16,1,128]{3,2,1,0:T(1,128)S(1)}, f32[16,16,1,128]{3,2,1,0:T(1,128)S(1)}, u32[]{:S(2)}, u32[]{:S(2)}) collective-permute-start(f32[16,16,1,128]{3,2,1,0:T(1,128)S(1)} %get-tuple-element.77), channel_id=1, source_target_pairs={{1,0},{2,1},{3,2},{4,3},{5,4},{6,5},{7,6},{9,8},{10,9},{11,10},{12... | collective-permute-start | bytes 393224 | tf_op jit(solution)/shard_map/ppermute | solution.py:20
  128.9 1.2 copy-start.12
  128.9 1.2 copy-start.30
  136.0 8.3 %collective-permute-start.12 = (f32[1,16,2,8,128]{4,1,0,3,2:T(8,128)S(1)}, f32[1,16,2,8,128]{4,1,0,3,2:T(8,128)S(1)}, u32[]{:S(2)}, u32[]{:S(2)}) collective-permute-start(f32[1,16,2,8,128]{4,1,0,3,2:T(8,128)S(1)} %get-tuple-element.43), channel_id=1, source_target_pairs={{0,32},{32,64},{64,96},{96,128},{128,160},{160,192},{192,224},{1,3... | collective-permute-start | bytes 393224 | tf_op jit(solution)/shard_map/ppermute | solution.py:18
  140.9 7.8 %collective-permute-start.13 = (f32[1,16,2,8,128]{4,1,0,3,2:T(8,128)S(1)}, f32[1,16,2,8,128]{4,1,0,3,2:T(8,128)S(1)}, u32[]{:S(2)}, u32[]{:S(2)}) collective-permute-start(f32[1,16,2,8,128]{4,1,0,3,2:T(8,128)S(1)} %get-tuple-element.44), channel_id=1, source_target_pairs={{32,0},{64,32},{96,64},{128,96},{160,128},{192,160},{224,192},{33,... | collective-permute-start | bytes 393224 | tf_op jit(solution)/shard_map/ppermute | solution.py:20
  148.9 4.4 collective-permute-start.14
  151.1 5.1 %collective-permute-start.15 = (f32[18,1,2,8,128]{4,1,0,3,2:T(1,128)S(1)}, f32[18,1,2,8,128]{4,1,0,3,2:T(1,128)S(1)}, u32[]{:S(2)}, u32[]{:S(2)}) collective-permute-start(f32[18,1,2,8,128]{4,1,0,3,2:T(1,128)S(1)} %get-tuple-element.28), channel_id=1, source_target_pairs={{8,0},{16,8},{24,16},{9,1},{17,9},{25,17},{10,2},{18,10},{26,18},{... | collective-permute-start | bytes 442376 | tf_op jit(solution)/shard_map/ppermute | solution.py:20
  158.0 10.5 %collective-permute-start.16 = (f32[16,16,1,128]{3,1,0,2:T(8,128)S(1)}, f32[16,16,1,128]{3,1,0,2:T(8,128)S(1)}, u32[]{:S(2)}, u32[]{:S(2)}) collective-permute-start(f32[16,16,1,128]{3,1,0,2:T(8,128)S(1)} %dynamic-slice_bitcast_fusion.1), channel_id=1, source_target_pairs={{0,1},{1,2},{2,3},{3,4},{4,5},{5,6},{6,7},{8,9},{9,10},{10,11},{11... | collective-permute-start | bytes 393224 | tf_op jit(solution)/shard_map/ppermute | solution.py:18
  168.6 6.9 %collective-permute-start.17 = (f32[16,16,1,128]{3,1,0,2:T(8,128)S(1)}, f32[16,16,1,128]{3,1,0,2:T(8,128)S(1)}, u32[]{:S(2)}, u32[]{:S(2)}) collective-permute-start(f32[16,16,1,128]{3,1,0,2:T(8,128)S(1)} %get-tuple-element.73), channel_id=1, source_target_pairs={{1,0},{2,1},{3,2},{4,3},{5,4},{6,5},{7,6},{9,8},{10,9},{11,10},{12... | collective-permute-start | bytes 393224 | tf_op jit(solution)/shard_map/ppermute | solution.py:20
  188.1 2.0 copy-start.2
  193.2 7.4 %collective-permute-start.18 = (f32[1,16,2,8,128]{4,1,0,3,2:T(8,128)S(1)}, f32[1,16,2,8,128]{4,1,0,3,2:T(8,128)S(1)}, u32[]{:S(2)}, u32[]{:S(2)}) collective-permute-start(f32[1,16,2,8,128]{4,1,0,3,2:T(8,128)S(1)} %get-tuple-element.35), channel_id=1, source_target_pairs={{0,32},{32,64},{64,96},{96,128},{128,160},{160,192},{192,224},{1,3... | collective-permute-start | bytes 393224 | tf_op jit(solution)/shard_map/ppermute | solution.py:18
  197.2 8.1 %collective-permute-start.19 = (f32[1,16,2,8,128]{4,1,0,3,2:T(8,128)S(1)}, f32[1,16,2,8,128]{4,1,0,3,2:T(8,128)S(1)}, u32[]{:S(2)}, u32[]{:S(2)}) collective-permute-start(f32[1,16,2,8,128]{4,1,0,3,2:T(8,128)S(1)} %get-tuple-element.36), channel_id=1, source_target_pairs={{32,0},{64,32},{96,64},{128,96},{160,128},{192,160},{224,192},{33,... | collective-permute-start | bytes 393224 | tf_op jit(solution)/shard_map/ppermute | solution.py:20
  205.5 4.0 collective-permute-start.20
  207.5 4.9 %collective-permute-start.21 = (f32[18,1,2,8,128]{4,1,0,3,2:T(1,128)S(1)}, f32[18,1,2,8,128]{4,1,0,3,2:T(1,128)S(1)}, u32[]{:S(2)}, u32[]{:S(2)}) collective-permute-start(f32[18,1,2,8,128]{4,1,0,3,2:T(1,128)S(1)} %get-tuple-element.26), channel_id=1, source_target_pairs={{8,0},{16,8},{24,16},{9,1},{17,9},{25,17},{10,2},{18,10},{26,18},{... | collective-permute-start | bytes 442376 | tf_op jit(solution)/shard_map/ppermute | solution.py:20
  214.3 10.5 %collective-permute-start.22 = (f32[16,16,1,128]{3,1,0,2:T(8,128)S(1)}, f32[16,16,1,128]{3,1,0,2:T(8,128)S(1)}, u32[]{:S(2)}, u32[]{:S(2)}) collective-permute-start(f32[16,16,1,128]{3,1,0,2:T(8,128)S(1)} %dynamic-slice_bitcast_fusion), channel_id=1, source_target_pairs={{0,1},{1,2},{2,3},{3,4},{4,5},{5,6},{6,7},{8,9},{9,10},{10,11},{11... | collective-permute-start | bytes 393224 | tf_op jit(solution)/shard_map/ppermute | solution.py:18
  224.9 6.9 %collective-permute-start.23 = (f32[16,16,1,128]{3,1,0,2:T(8,128)S(1)}, f32[16,16,1,128]{3,1,0,2:T(8,128)S(1)}, u32[]{:S(2)}, u32[]{:S(2)}) collective-permute-start(f32[16,16,1,128]{3,1,0,2:T(8,128)S(1)} %get-tuple-element.71), channel_id=1, source_target_pairs={{1,0},{2,1},{3,2},{4,3},{5,4},{6,5},{7,6},{9,8},{10,9},{11,10},{12... | collective-permute-start | bytes 393224 | tf_op jit(solution)/shard_map/ppermute | solution.py:20
  233.3 1.2 copy-start.22
  234.5 1.5 copy-start.32
  237.6 1.7 copy-start.9
  239.3 1.5 copy-start.33
  242.4 1.8 copy-start.31
  245.1 1.7 copy-start.18
  246.8 1.2 copy-start.16
  249.2 209.3 %all-reduce.51.cloned.1.call-start = ((), (), s32[]{:S(2)}) async-start(), calls=%async_computation.1 | async-start | bytes 1310720 | tf_op jit(solution)/shard_map/psum | solution.py:255
  249.3 206.1 %copy-start.4 = (bf16[16,16,2,8,128]{4,3,2,1,0:T(8,128)(2,1)S(1)}, bf16[16,16,2,8,128]{4,3,2,1,0:T(8,128)(2,1)}, u32[]{:S(2)}) copy-start(bf16[16,16,2,8,128]{4,3,2,1,0:T(8,128)(2,1)} %copy-done.3) | copy-start | bytes 3145732
  (12 other events, 11.6 us)
Sparse Core Ops, SparseCore 0:
  249.3 111.6 all-reduce.48
  363.6 74.7 all-reduce.50
